TPU v7x, 32 devices: a whole 2x2x4 slice. The times are simulated.
32 devices in a mesh: row: 2 (over x), col: 4 (over z), box: 4 (over y, core).
Axes of the slice: x: 2, y: 2, z: 4, core: 2. Of those that a mesh axis runs over, the one named last changes fastest.
Arguments:
- coeffs: bfloat16 [81920, 512], P(('row', 'box'), 'col'), may hold values from -6 to 6
- reflectors: bfloat16 [81920, 256], P(('row', 'box')), may hold values from -0.078125 to 0.078125
- factor: float32 [256, 256], replicated, may hold values from -0.375 to 0.375
- func_exp: float32 [81920], replicated, may hold values from 0.5 to 20
- func_atom: int32 [81920], replicated, may hold values from 0 to 8191, never falling along the last dimension, each value on 1 to 20 neighbouring positions
- atom_pos: float32 [3, 8192], replicated, may hold values from 0 to 1
- point_pos: float32 [3, 128, 128], P(None, ('row', 'col', 'box')), may hold values from 0 to 1
- send_tiles: int32 [8, 8, 2], replicated, may hold values from 0 to 79, as said below
- box_tiles: int32 [128, 16], P(('row', 'col', 'box')), may hold values from 0 to 15, as said below
- box_count: int32 [128], P(('row', 'col', 'box')), may hold values from 1 to 16
Outputs:
- rotated: bfloat16 [81920, 512], P(('row', 'box'), 'col')
- density: float32 [128, 128], P(('row', 'col', 'box'))
Inputs may be any that keep to these rules, and one draw needn't show every extreme that they name: `send_tiles`: for each basis group and box group the 2 tiles are different local tiles of the basis group. `box_tiles`: the 16 slots listed by a box are different. `func_atom`: never falls along the basis functions; every atom carries 1 to 20 functions.
All inputs are finite; a program needn't handle non-finite values.
Results may differ from a plain program's by a relative error of at most 0.015.
Values may be sent and summed in bfloat16 or wider, within the bound.
A program may use at most 128 MiB of HBM per device.

v0:
```python
import math
import jax
import jax.numpy as jnp
from jax import lax
from jax.sharding import PartitionSpec as P

K = 512
TILE = 128


def box_density(arrived, slot_alpha, slot_centre, listed, count, points):
    alpha = slot_alpha[listed]
    centre = slot_centre[:, listed]
    first = points[0][:, None, None] - centre[0][None]
    dist = first * first
    second = points[1][:, None, None] - centre[1][None]
    dist = dist + second * second
    third = points[2][:, None, None] - centre[2][None]
    dist = dist + third * third
    live = jnp.arange(listed.shape[0], dtype=jnp.int32) < count
    phi = jnp.where(live[None, :, None], jnp.exp(-alpha[None] * dist), 0.0).astype(jnp.bfloat16)
    phi = phi.reshape(points.shape[1], -1)
    block = arrived[listed].reshape(-1, arrived.shape[2])
    orbital = jnp.dot(phi, block, preferred_element_type=jnp.float32)
    return jnp.sum(orbital * orbital, 1) / (K * TILE)


def by_blocks(arrived, slot_alpha, slot_centre, lists, counts, points):
    boxes = lists.shape[0]
    width = math.gcd(boxes, 2)
    steps = boxes // width
    lists_blocked = lists.reshape(steps, width, lists.shape[1])
    counts_blocked = counts.reshape(steps, width)
    moved = jnp.moveaxis(points, 1, 0)
    points_blocked = moved.reshape(steps, width, moved.shape[1], moved.shape[2])
    single = jax.vmap(
        lambda listed, count, where: box_density(
            arrived, slot_alpha, slot_centre, listed, count, where
        )
    )

    def one_block(items):
        return single(items[0], items[1], items[2])

    result = lax.map(one_block, (lists_blocked, counts_blocked, points_blocked))
    return result.reshape(boxes, result.shape[2])


def per_device(
    coeffs,
    reflectors,
    factor,
    func_exp,
    func_atom,
    atom_pos,
    point_pos,
    send_tiles,
    box_tiles,
    box_count,
):
    panel_part = jnp.dot(reflectors.T, coeffs, preferred_element_type=jnp.float32)
    panel = lax.psum(panel_part.astype(jnp.bfloat16), ("row", "box")).astype(jnp.float32)
    scaled = jnp.dot(factor, panel, precision=lax.Precision.HIGHEST).astype(jnp.bfloat16)
    rotated = (
        coeffs.astype(jnp.float32) - jnp.dot(reflectors, scaled, preferred_element_type=jnp.float32)
    ).astype(jnp.bfloat16)
    peers = lax.axis_size(("row", "box"))
    group = lax.axis_index(("row", "box"))
    capacity = send_tiles.shape[2]
    local_tiles = coeffs.shape[0] // TILE
    slots = jnp.arange(peers * capacity, dtype=jnp.int32)
    source = slots // capacity
    within = slots % capacity
    tile = source * local_tiles + send_tiles[source, group, within]
    funcs = tile[:, None] * TILE + jnp.arange(TILE, dtype=jnp.int32)[None, :]
    slot_alpha = func_exp[funcs]
    slot_centre = atom_pos[:, func_atom[funcs]]
    outgoing_index = send_tiles[group]
    outgoing = rotated.reshape(local_tiles, TILE, rotated.shape[1])[outgoing_index]
    arrived = lax.all_to_all(outgoing, ("row", "box"), split_axis=0, concat_axis=0, tiled=True)
    arrived = arrived.reshape(peers * capacity, TILE, arrived.shape[3])
    lists, counts = (
        lax.all_gather(box_tiles, "col", axis=0, tiled=True),
        lax.all_gather(box_count, "col", axis=0, tiled=True),
    )
    points = lax.all_gather(point_pos, "col", axis=1, tiled=True)
    partial_value = by_blocks(arrived, slot_alpha, slot_centre, lists, counts, points)
    density = lax.psum_scatter(
        partial_value.astype(jnp.bfloat16), "col", scatter_dimension=0, tiled=True
    ).astype(jnp.float32)
    return (rotated, density)


def solution(mesh):
    in_specs = (
        P(("row", "box"), "col"),
        P(("row", "box"), None),
        P(),
        P(),
        P(),
        P(),
        P(None, ("row", "col", "box"), None),
        P(),
        P(("row", "col", "box"), None),
        P(("row", "col", "box")),
    )
    out_specs = (P(("row", "box"), "col"), P(("row", "col", "box"), None))
    return jax.shard_map(
        per_device, mesh=mesh, in_specs=in_specs, out_specs=out_specs, check_vma=False
    )
```

profile of v0, /device:TPU:0, one launch (start us, length us, event | category | flops | bytes accessed | tf_op | source)
XLA Modules:
  0.0 196.5 jit_solution(6431484893824231304)
XLA Ops:
  7.2 5.5 %convolution_convert_fusion = bf16[256,128]{1,0:T(8,128)(2,1)} fusion(bf16[10240,256]{1,0:T(8,128)(2,1)} %param.13, bf16[10240,128]{1,0:T(8,128)(2,1)} %param.12), kind=kOutput, calls=%fused_computation.42 | convolution fusion | flops 671121408 | bytes 7929856 | tf_op jit(solution)/shard_map/dot_general | solution.py:61
  12.9 0.7 gather_fusion.3
  13.8 3.0 %copy.28 = bf16[10240,128]{0,1:T(8,128)(2,1)S(1)} copy(bf16[10240,128]{1,0:T(8,128)(2,1)} %param.12) | data formatting | bytes 5242880 | tf_op args[0]
  16.8 2.6 %copy.31 = f32[3,8192]{0,1:T(8,128)} copy(f32[3,8192]{1,0:T(4,128)S(1)} %copy-done.5) | data formatting | bytes 196608 | tf_op args[5]
  19.4 48.7 %all-reduce.4.cloned.1.call-done = bf16[256,128]{1,0:T(8,128)(2,1)} async-done(((bf16[256,128]{1,0:T(8,128)(2,1)}), bf16[256,128]{1,0:T(8,128)(2,1)}) %all-reduce.4.cloned.1.call-update) | async-done | bytes 65552 | tf_op jit(solution)/shard_map/psum | solution.py:62
  68.1 1.1 convolution_convert_fusion.1
  69.3 5.8 %fusion.13 = bf16[10240,128]{0,1:T(8,128)(2,1)} fusion(bf16[128,256]{1,0:T(8,128)(2,1)S(1)} %convolution_convert_fusion.1, bf16[10240,256]{1,0:T(8,128)(2,1)} %param.13, bf16[10240,128]{0,1:T(8,128)(2,1)S(1)} %copy.28), kind=kOutput, calls=%fused_computation.41 | convolution fusion | flops 675020800 | bytes 10551296 | tf_op jit(solution)/shard_map/dot_general | solution.py:65
  75.1 3.2 %copy.36 = bf16[10240,128]{1,0:T(8,128)(2,1)S(1)} copy(bf16[10240,128]{0,1:T(8,128)(2,1)} %fusion.13) | data formatting | bytes 5242880
  78.3 1.6 gather_fusion.7
  80.0 3.5 %all-to-all-start = ((bf16[8,2,128,128]{3,2,1,0:T(8,128)(2,1)}), bf16[8,2,128,128]{3,2,1,0:T(8,128)(2,1)S(1)}, u32[]{:S(2)}, u32[]{:S(2)}) async-start(bf16[8,2,128,128]{3,2,1,0:T(8,128)(2,1)} %bitcast.116), calls=%async_computation | async-start | bytes 1048576 | tf_op jit(solution)/shard_map/all_to_all | solution.py:80
  83.6 11.8 %gather_fusion.5 = s32[2048]{0:T(1024)S(1)} fusion(s32[81920]{0:T(1024)S(1)} %copy-done, s32[2048]{0:T(1024)S(1)} %fusion.15), kind=kCustom, calls=%fused_computation.5 | custom fusion | bytes 24576 | tf_op jit(solution)/shard_map/gather | solution.py:77
  95.4 7.7 %gather_fusion.6 = f32[2048,3]{1,0:T(8,128)S(1)} fusion(f32[3,8192]{0,1:T(8,128)} %copy.31, s32[2048]{0:T(1024)S(1)} %fusion.17), kind=kCustom, calls=%fused_computation.6 | custom fusion | bytes 57344 | tf_op jit(solution)/shard_map/gather | solution.py:77
  103.4 11.8 %gather_fusion.4 = f32[2048]{0:T(1024)S(1)} fusion(f32[81920]{0:T(1024)S(1)} %copy-done.1, s32[2048]{0:T(1024)S(1)} %fusion.15), kind=kCustom, calls=%fused_computation.4 | custom fusion | bytes 24576 | tf_op jit(solution)/shard_map/gather | solution.py:76
  115.3 0.7 fusion.28
  116.8 8.3 %all-reduce = s32[16]{0:T(128)S(1)} all-reduce(s32[16]{0:T(128)S(1)} %dynamic-update-slice), channel_id=1, replica_groups=mesh['row'=2,'col'=4,'box'=4] {'col'}, use_global_device_ids=true, to_apply=%add | all-reduce | flops 16 | bytes 128
  125.1 13.1 %all_gather.11 = f32[3,16,128]{2,0,1:T(4,128)S(1)} all-gather(f32[3,4,128]{2,0,1:T(4,128)S(1)} %copy.29), channel_id=1, replica_groups=mesh['row'=2,'col'=4,'box'=4] {'col'}, dimensions={1}, use_global_device_ids=true | all-gather | bytes 30720 | tf_op jit(solution)/shard_map/all_gather | solution.py:86
  138.9 11.9 %all-gather = s32[4,4,16]{2,1,0:T(4,128)S(1)} all-gather(s32[1,4,16]{2,1,0:T(4,128)S(1)} %bitcast.126), channel_id=1, replica_groups=mesh['row'=2,'col'=4,'box'=4] {'col'}, dimensions={0}, use_global_device_ids=true | all-gather | bytes 1280 | tf_op jit(solution)/shard_map/all_gather | solution.py:83
  150.8 29.7 %while.10 = (s32[]{:T(128)}, bf16[8,2,128]{2,1,0:T(2,128)(2,1)S(1)}, s32[8,2]{1,0:T(8,128)S(1)}, s32[8,2,16]{2,1,0:T(2,128)S(1)}, f32[16,128]{1,0:T(8,128)S(1)},...) while((s32[]{:T(128)}, ...), condition=%wide.region_3.4_spmd, body=%wide.region_1.3_spmd.sunk | while | flops 140055680 | bytes 3644613 | solution.py:45
  150.9 0.6 gather_fusion.1
  151.7 0.7 gather_fusion
  152.5 0.6 gather_fusion.2
  153.3 1.2 fusion.41
  154.6 0.6 gather_fusion.1
  155.4 0.7 gather_fusion
  156.2 0.6 gather_fusion.2
  157.0 1.2 fusion.41
  158.3 0.6 gather_fusion.1
  159.1 0.7 gather_fusion
  160.7 1.2 fusion.41
  162.1 0.6 gather_fusion.1
  162.8 0.7 gather_fusion
  163.6 0.6 gather_fusion.2
  164.4 1.2 fusion.41
  165.8 0.6 gather_fusion.1
  166.5 0.7 gather_fusion
  167.3 0.6 gather_fusion.2
  168.1 1.2 fusion.41
  169.5 0.6 gather_fusion.1
  170.3 0.7 gather_fusion
  171.8 1.2 fusion.41
  173.2 0.6 gather_fusion.1
  174.0 0.7 gather_fusion
  175.5 1.2 fusion.41
  176.9 0.6 gather_fusion.1
  177.7 0.7 gather_fusion
  179.3 1.2 fusion.41
  180.5 8.6 %all-reduce.1 = bf16[16,128]{1,0:T(8,128)(2,1)S(1)} all-reduce(bf16[16,128]{1,0:T(8,128)(2,1)S(1)} %bitcast.125), channel_id=2, replica_groups=mesh['row'=2,'col'=4,'box'=4] {'col'}, use_global_device_ids=true, to_apply=%region_4.5.clone | all-reduce | flops 2048 | bytes 8192
  189.1 0.6 dynamic-slice_convert_fusion
  (162 shorter events, 7.2 us)
Async XLA Ops:
  7.2 76.4 %copy-start = (s32[81920]{0:T(1024)S(1)}, s32[81920]{0:T(1024)}, u32[]{:S(2)}) copy-start(s32[81920]{0:T(1024)} %param.16) | copy-start | bytes 983044
  7.2 5.7 %copy-start.2 = (s32[8,8,2]{1,2,0:T(2,128)S(1)}, s32[8,8,2]{1,2,0:T(2,128)}, u32[]{:S(2)}) copy-start(s32[8,8,2]{1,2,0:T(2,128)} %param.19) | copy-start | bytes 1540
  7.2 60.9 %all-reduce.4.cloned.1.call-start = ((), (), s32[]{:S(2)}) async-start(), calls=%async_computation.1 | async-start | bytes 131072 | tf_op jit(solution)/shard_map/psum | solution.py:62
  13.7 3.1 %copy-start.5 = (f32[3,8192]{1,0:T(4,128)S(1)}, f32[3,8192]{1,0:T(4,128)}, u32[]{:S(2)}) copy-start(f32[3,8192]{1,0:T(4,128)} %param.17) | copy-start | bytes 294916
  16.8 51.3 %copy-start.4 = (f32[256,256]{1,0:T(8,128)S(1)}, f32[256,256]{1,0:T(8,128)}, u32[]{:S(2)}) copy-start(f32[256,256]{1,0:T(8,128)} %param.14) | copy-start | bytes 786436
  78.3 5.2 %copy-start.3 = (bf16[10240,128]{1,0:T(8,128)(2,1)}, bf16[10240,128]{1,0:T(8,128)(2,1)S(1)}, u32[]{:S(2)}) copy-start(bf16[10240,128]{1,0:T(8,128)(2,1)S(1)} %copy.36) | copy-start | bytes 7864324
  80.0 70.8 %all-to-all-start = ((bf16[8,2,128,128]{3,2,1,0:T(8,128)(2,1)}), bf16[8,2,128,128]{3,2,1,0:T(8,128)(2,1)S(1)}, u32[]{:S(2)}, u32[]{:S(2)}) async-start(bf16[8,2,128,128]{3,2,1,0:T(8,128)(2,1)} %bitcast.116), calls=%async_computation | async-start | bytes 1048576 | tf_op jit(solution)/shard_map/all_to_all | solution.py:80
  95.4 8.1 %copy-start.1 = (f32[81920]{0:T(1024)S(1)}, f32[81920]{0:T(1024)}, u32[]{:S(2)}) copy-start(f32[81920]{0:T(1024)} %param.15) | copy-start | bytes 983044
  103.4 11.8 %copy-start.8 = (u32[32]{0:T(128)S(1)}, u32[32]{0:T(128)}, u32[]{:S(2)}) copy-start(u32[32]{0:T(128)} %constant.107) | copy-start | bytes 388
  103.4 13.1 %copy-start.9 = (s32[4]{0:T(128)S(1)}, s32[4]{0:T(128)}, u32[]{:S(2)}) copy-start(s32[4]{0:T(128)} %param.21) | copy-start | bytes 52
  103.4 21.7 %copy-start.6 = (f32[3,4,128]{2,1,0:T(4,128)S(1)}, f32[3,4,128]{2,1,0:T(4,128)}, u32[]{:S(2)}) copy-start(f32[3,4,128]{2,1,0:T(4,128)} %param.18) | copy-start | bytes 18436
  103.4 35.5 %copy-start.7 = (s32[4,16]{1,0:T(4,128)S(1)}, s32[4,16]{1,0:T(4,128)}, u32[]{:S(2)}) copy-start(s32[4,16]{1,0:T(4,128)} %param.20) | copy-start | bytes 772
Sparse Core Ops, SparseCore 0:
  12.9 55.1 all-reduce.3
where the time goes:
time: 197 us
  local copies, waits for them, and re-layouts  62.4 us (32%)
  waiting for transfers between devices  48.7 us (25%)
  blocking collectives  41.9 us (21%)
  matrix products  22.2 us (11%)
  between operations  15.6 us (8%)
  starting transfers between devices  3.53 us (2%)
    psum x1, waiting for transfers between devices, per_device(): lax.psum(panel_part.astype(jnp.bfloat16), ('row', 'box'))  48.7 us
    gather x3, local copies, waits for them, and re-layouts, per_device(): slot_centre = atom_pos[:, func_atom[funcs]]  19.8 us
    unnamed x2, blocking collectives  16.9 us
    all_gather x1, blocking collectives, per_device(): points = lax.all_gather(point_pos, 'col', axis=1, tiled=True)  13.1 us
    all_gather x1, blocking collectives, per_device(): lax.all_gather(box_tiles, 'col', axis=0, tiled=True)  11.9 us
    gather x1, local copies, waits for them, and re-layouts, per_device(): slot_alpha = func_exp[funcs]  11.8 us
    unnamed x27, local copies, waits for them, and re-layouts  9.83 us
    dot_general x8, matrix products, box_density(): orbital = jnp.dot(phi, block, preferred_element_type=jnp.float32)  9.66 us
  transfers between devices with their start and end apart: 2, of which 1 were waited for; matrix products, arithmetic and copies ran while one was open for 20% of the time, Pallas kernels for 0%

commit v1 on v0

--- a/solution.py
+++ b/solution.py
@@ -83,7 +83,23 @@
         lax.all_gather(box_tiles, "col", axis=0, tiled=True),
         lax.all_gather(box_count, "col", axis=0, tiled=True),
     )
-    points = lax.all_gather(point_pos, "col", axis=1, tiled=True)
+    n_shards = jax.lax.axis_size("col")
+    all_rows = []
+    for it in [*range(n_shards)]:
+        all_rows.append((it, (it + 1) % n_shards))
+    store = []
+    for it in tuple(range(n_shards)):
+        store.append((it, (it - 1) % n_shards))
+    mat_out, formed = ([point_pos], [point_pos])
+    for _ in range(n_shards // 2):
+        res = jax.lax.ppermute(mat_out[-1], "col", all_rows)
+        mat_out.append(res)
+    for _ in [*range((n_shards - 1) // 2)]:
+        formed.append(jax.lax.ppermute(formed[-1], "col", store))
+    next_value = jnp.concatenate([*mat_out[::-1], *formed[1:]], axis=1)
+    points = jnp.roll(
+        next_value, (jax.lax.axis_index("col") - n_shards // 2) * point_pos.shape[1], axis=1
+    )
     partial_value = by_blocks(arrived, slot_alpha, slot_centre, lists, counts, points)
     density = lax.psum_scatter(
         partial_value.astype(jnp.bfloat16), "col", scatter_dimension=0, tiled=True

time: 197 us -> 191 us (0.970)
  blocking collectives: 41.9 us -> 28.7 us
  starting transfers between devices: 3.53 us -> 10.2 us
    all_gather x1 -> x0, blocking collectives: 13.1 us -> none  [per_device(): points = lax.all_gather(point_pos, 'col', axis=1, tiled=True)]
    ppermute x0 -> x3, starting transfers between devices: none -> 6.71 us  [the longest x2 4.61 us: per_device(): res = jax.lax.ppermute(mat_out[-1], 'col', all_rows)]
    unnamed x27 -> x24, local copies, waits for them, and re-layouts: 9.83 us -> 10.7 us
  transfers between devices with their start and end apart: 2 -> 5, of which waited for: 1 -> 1; matrix products, arithmetic and copies ran while one was open for 20% -> 30% of each run, Pallas kernels for 0% -> 0%
where the time goes in v1:
time: 191 us
  local copies, waits for them, and re-layouts  63.3 us (33%)
  waiting for transfers between devices  48.3 us (25%)
  blocking collectives  28.7 us (15%)
  matrix products  22.1 us (12%)
  between operations  15.6 us (8%)
  starting transfers between devices  10.2 us (5%)
    psum x1, waiting for transfers between devices, per_device(): lax.psum(panel_part.astype(jnp.bfloat16), ('row', 'box'))  48.2 us
    gather x3, local copies, waits for them, and re-layouts, per_device(): slot_centre = atom_pos[:, func_atom[funcs]]  19.8 us
    unnamed x2, blocking collectives  16.8 us
    all_gather x1, blocking collectives, per_device(): lax.all_gather(box_tiles, 'col', axis=0, tiled=True)  11.9 us
    gather x1, local copies, waits for them, and re-layouts, per_device(): slot_alpha = func_exp[funcs]  11.8 us
    unnamed x24, local copies, waits for them, and re-layouts  10.7 us
    dot_general x8, matrix products, box_density(): orbital = jnp.dot(phi, block, preferred_element_type=jnp.float32)  9.66 us
    gather x8, local copies, waits for them, and re-layouts, box_density(): block = arrived[listed].reshape(-1, arrived.shape[2])  5.99 us
  transfers between devices with their start and end apart: 5, of which 1 were waited for; matrix products, arithmetic and copies ran while one was open for 30% of the time, Pallas kernels for 0%

profile of v1, /device:TPU:0, one launch (start us, length us, event | category | flops | bytes accessed | tf_op | source)
XLA Modules:
  0.0 190.5 jit_solution(9481398206345519462)
XLA Ops:
  7.2 3.1 %collective-permute-start = (f32[3,4,128]{2,1,0:T(4,128)}, f32[3,4,128]{2,1,0:T(4,128)S(1)}, u32[]{:S(2)}, u32[]{:S(2)}) collective-permute-start(f32[3,4,128]{2,1,0:T(4,128)} %param.18), channel_id=1, source_target_pairs={{0,4},{4,8},{8,12},{12,0},{1,5},{5,9},{9,13},{13,1},{2,6},{6,10},{... | collective-permute-start | bytes 18440 | tf_op jit(solution)/shard_map/ppermute | solution.py:95
  10.3 2.1 %collective-permute-start.2 = (f32[3,4,128]{2,1,0:T(4,128)}, f32[3,4,128]{2,1,0:T(4,128)S(1)}, u32[]{:S(2)}, u32[]{:S(2)}) collective-permute-start(f32[3,4,128]{2,1,0:T(4,128)} %param.18), channel_id=1, source_target_pairs={{0,12},{4,0},{8,4},{12,8},{1,13},{5,1},{9,5},{13,9},{2,14},{6,2},{... | collective-permute-start | bytes 18440 | tf_op jit(solution)/shard_map/ppermute | solution.py:98
  12.4 5.5 %convolution_convert_fusion = bf16[256,128]{1,0:T(8,128)(2,1)} fusion(bf16[10240,256]{1,0:T(8,128)(2,1)} %param.13, bf16[10240,128]{1,0:T(8,128)(2,1)} %param.12), kind=kOutput, calls=%fused_computation.42 | convolution fusion | flops 671121408 | bytes 7929856 | tf_op jit(solution)/shard_map/dot_general | solution.py:61
  18.0 0.7 gather_fusion.3
  18.9 3.0 %copy.28 = bf16[10240,128]{0,1:T(8,128)(2,1)S(1)} copy(bf16[10240,128]{1,0:T(8,128)(2,1)} %param.12) | data formatting | bytes 5242880 | tf_op args[0]
  21.9 48.2 %all-reduce.4.cloned.1.call-done = bf16[256,128]{1,0:T(8,128)(2,1)} async-done(((bf16[256,128]{1,0:T(8,128)(2,1)}), bf16[256,128]{1,0:T(8,128)(2,1)}) %all-reduce.4.cloned.1.call-update) | async-done | bytes 65552 | tf_op jit(solution)/shard_map/psum | solution.py:62
  70.2 1.1 convolution_convert_fusion.1
  71.3 5.8 %fusion.13 = bf16[10240,128]{0,1:T(8,128)(2,1)} fusion(bf16[128,256]{1,0:T(8,128)(2,1)S(1)} %convolution_convert_fusion.1, bf16[10240,256]{1,0:T(8,128)(2,1)} %param.13, bf16[10240,128]{0,1:T(8,128)(2,1)S(1)} %copy.28), kind=kOutput, calls=%fused_computation.41 | convolution fusion | flops 675020800 | bytes 10551296 | tf_op jit(solution)/shard_map/dot_general | solution.py:65
  77.1 3.2 %copy.34 = bf16[10240,128]{1,0:T(8,128)(2,1)S(1)} copy(bf16[10240,128]{0,1:T(8,128)(2,1)} %fusion.13) | data formatting | bytes 5242880
  80.4 1.6 gather_fusion.7
  82.0 3.5 %all-to-all-start = ((bf16[8,2,128,128]{3,2,1,0:T(8,128)(2,1)}), bf16[8,2,128,128]{3,2,1,0:T(8,128)(2,1)S(1)}, u32[]{:S(2)}, u32[]{:S(2)}) async-start(bf16[8,2,128,128]{3,2,1,0:T(8,128)(2,1)} %bitcast.116), calls=%async_computation | async-start | bytes 1048576 | tf_op jit(solution)/shard_map/all_to_all | solution.py:80
  85.6 11.8 %gather_fusion.5 = s32[2048]{0:T(1024)S(1)} fusion(s32[81920]{0:T(1024)S(1)} %copy-done, s32[2048]{0:T(1024)S(1)} %fusion.15), kind=kCustom, calls=%fused_computation.5 | custom fusion | bytes 24576 | tf_op jit(solution)/shard_map/gather | solution.py:77
  97.4 1.5 collective-permute-start.1
  99.0 3.5 %copy.29 = f32[3,8192]{0,1:T(8,128)} copy(f32[3,8192]{1,0:T(4,128)} %param.17) | data formatting | bytes 196608 | tf_op args[5]
  102.5 7.6 %gather_fusion.6 = f32[2048,3]{1,0:T(8,128)S(1)} fusion(f32[3,8192]{0,1:T(8,128)} %copy.29, s32[2048]{0:T(1024)S(1)} %fusion.17), kind=kCustom, calls=%fused_computation.6 | custom fusion | bytes 57344 | tf_op jit(solution)/shard_map/gather | solution.py:77
  110.5 11.8 %gather_fusion.4 = f32[2048]{0:T(1024)S(1)} fusion(f32[81920]{0:T(1024)S(1)} %copy-done.1, s32[2048]{0:T(1024)S(1)} %fusion.15), kind=kCustom, calls=%fused_computation.4 | custom fusion | bytes 24576 | tf_op jit(solution)/shard_map/gather | solution.py:76
  122.3 0.7 fusion.28
  123.8 8.3 %all-reduce = s32[16]{0:T(128)S(1)} all-reduce(s32[16]{0:T(128)S(1)} %dynamic-update-slice), channel_id=1, replica_groups=mesh['row'=2,'col'=4,'box'=4] {'col'}, use_global_device_ids=true, to_apply=%add | all-reduce | flops 16 | bytes 128
  132.8 11.9 %all-gather = s32[4,4,16]{2,1,0:T(4,128)S(1)} all-gather(s32[1,4,16]{2,1,0:T(4,128)S(1)} %bitcast.126), channel_id=1, replica_groups=mesh['row'=2,'col'=4,'box'=4] {'col'}, dimensions={0}, use_global_device_ids=true | all-gather | bytes 1280 | tf_op jit(solution)/shard_map/all_gather | solution.py:83
  144.8 29.7 %while.10 = (s32[]{:T(128)}, bf16[8,2,128]{2,1,0:T(2,128)(2,1)S(1)}, s32[8,2]{1,0:T(8,128)S(1)}, s32[8,2,16]{2,1,0:T(2,128)S(1)}, f32[16,128]{1,0:T(8,128)S(1)},...) while((s32[]{:T(128)}, ...), condition=%wide.region_3.4_spmd, body=%wide.region_1.3_spmd.sunk | while | flops 140055680 | bytes 3644613 | solution.py:45
  144.9 0.6 gather_fusion.1
  145.7 0.7 gather_fusion
  146.5 0.6 gather_fusion.2
  147.3 1.2 fusion.41
  148.7 0.6 gather_fusion.1
  149.4 0.7 gather_fusion
  150.2 0.6 gather_fusion.2
  151.0 1.2 fusion.41
  152.4 0.6 gather_fusion.1
  153.2 0.7 gather_fusion
  154.7 1.2 fusion.41
  156.1 0.6 gather_fusion.1
  156.9 0.7 gather_fusion
  158.4 1.2 fusion.41
  159.8 0.6 gather_fusion.1
  160.6 0.7 gather_fusion
  162.2 1.2 fusion.41
  163.5 0.6 gather_fusion.1
  164.3 0.7 gather_fusion
  165.9 1.2 fusion.41
  167.2 0.6 gather_fusion.1
  168.0 0.7 gather_fusion
  169.6 1.2 fusion.41
  170.9 0.6 gather_fusion.1
  171.7 0.7 gather_fusion
  173.3 1.2 fusion.41
  174.5 8.6 %all-reduce.1 = bf16[16,128]{1,0:T(8,128)(2,1)S(1)} all-reduce(bf16[16,128]{1,0:T(8,128)(2,1)S(1)} %bitcast.125), channel_id=2, replica_groups=mesh['row'=2,'col'=4,'box'=4] {'col'}, use_global_device_ids=true, to_apply=%region_4.5.clone | all-reduce | flops 2048 | bytes 8192
  183.1 0.6 dynamic-slice_convert_fusion
  (165 shorter events, 8.4 us)
Async XLA Ops:
  7.2 78.4 %copy-start = (s32[81920]{0:T(1024)S(1)}, s32[81920]{0:T(1024)}, u32[]{:S(2)}) copy-start(s32[81920]{0:T(1024)} %param.16) | copy-start | bytes 983044
  7.2 10.8 %copy-start.2 = (s32[8,8,2]{1,2,0:T(2,128)S(1)}, s32[8,8,2]{1,2,0:T(2,128)}, u32[]{:S(2)}) copy-start(s32[8,8,2]{1,2,0:T(2,128)} %param.19) | copy-start | bytes 1540
  7.2 63.0 %all-reduce.4.cloned.1.call-start = ((), (), s32[]{:S(2)}) async-start(), calls=%async_computation.1 | async-start | bytes 131072 | tf_op jit(solution)/shard_map/psum | solution.py:62
  7.2 90.2 %collective-permute-start = (f32[3,4,128]{2,1,0:T(4,128)}, f32[3,4,128]{2,1,0:T(4,128)S(1)}, u32[]{:S(2)}, u32[]{:S(2)}) collective-permute-start(f32[3,4,128]{2,1,0:T(4,128)} %param.18), channel_id=1, source_target_pairs={{0,4},{4,8},{8,12},{12,0},{1,5},{5,9},{9,13},{13,1},{2,6},{6,10},{... | collective-permute-start | bytes 18440 | tf_op jit(solution)/shard_map/ppermute | solution.py:95
  10.3 134.4 %collective-permute-start.2 = (f32[3,4,128]{2,1,0:T(4,128)}, f32[3,4,128]{2,1,0:T(4,128)S(1)}, u32[]{:S(2)}, u32[]{:S(2)}) collective-permute-start(f32[3,4,128]{2,1,0:T(4,128)} %param.18), channel_id=1, source_target_pairs={{0,12},{4,0},{8,4},{12,8},{1,13},{5,1},{9,5},{13,9},{2,14},{6,2},{... | collective-permute-start | bytes 18440 | tf_op jit(solution)/shard_map/ppermute | solution.py:98
  18.9 51.3 %copy-start.4 = (f32[256,256]{1,0:T(8,128)S(1)}, f32[256,256]{1,0:T(8,128)}, u32[]{:S(2)}) copy-start(f32[256,256]{1,0:T(8,128)} %param.14) | copy-start | bytes 786436
  80.4 17.0 %copy-start.3 = (bf16[10240,128]{1,0:T(8,128)(2,1)}, bf16[10240,128]{1,0:T(8,128)(2,1)S(1)}, u32[]{:S(2)}) copy-start(bf16[10240,128]{1,0:T(8,128)(2,1)S(1)} %copy.34) | copy-start | bytes 7864324
  82.0 62.8 %all-to-all-start = ((bf16[8,2,128,128]{3,2,1,0:T(8,128)(2,1)}), bf16[8,2,128,128]{3,2,1,0:T(8,128)(2,1)S(1)}, u32[]{:S(2)}, u32[]{:S(2)}) async-start(bf16[8,2,128,128]{3,2,1,0:T(8,128)(2,1)} %bitcast.116), calls=%async_computation | async-start | bytes 1048576 | tf_op jit(solution)/shard_map/all_to_all | solution.py:80
  97.4 47.3 %collective-permute-start.1 = (f32[3,4,128]{2,1,0:T(4,128)S(1)}, f32[3,4,128]{2,1,0:T(4,128)S(1)}, u32[]{:S(2)}, u32[]{:S(2)}) collective-permute-start(f32[3,4,128]{2,1,0:T(4,128)S(1)} %collective-permute-done), channel_id=1, source_target_pairs={{0,4},{4,8},{8,12},{12,0},{1,5},{5,9},{9,13},{13,1},{2,6},{6,10},{... | collective-permute-start | bytes 18440 | tf_op jit(solution)/shard_map/ppermute | solution.py:95
  99.0 11.5 %copy-start.1 = (f32[81920]{0:T(1024)S(1)}, f32[81920]{0:T(1024)}, u32[]{:S(2)}) copy-start(f32[81920]{0:T(1024)} %param.15) | copy-start | bytes 983044
  110.4 11.8 %copy-start.7 = (u32[32]{0:T(128)S(1)}, u32[32]{0:T(128)}, u32[]{:S(2)}) copy-start(u32[32]{0:T(128)} %constant.133) | copy-start | bytes 388
  110.4 13.2 %copy-start.8 = (s32[4]{0:T(128)S(1)}, s32[4]{0:T(128)}, u32[]{:S(2)}) copy-start(s32[4]{0:T(128)} %param.21) | copy-start | bytes 52
  110.4 22.4 %copy-start.6 = (s32[4,16]{1,0:T(4,128)S(1)}, s32[4,16]{1,0:T(4,128)}, u32[]{:S(2)}) copy-start(s32[4,16]{1,0:T(4,128)} %param.20) | copy-start | bytes 772
  110.5 34.3 %copy-start.5 = (f32[3,4,128]{2,1,0:T(4,128)S(1)}, f32[3,4,128]{2,1,0:T(4,128)}, u32[]{:S(2)}) copy-start(f32[3,4,128]{2,1,0:T(4,128)} %param.18) | copy-start | bytes 18436
Sparse Core Ops, SparseCore 0:
  18.1 52.0 all-reduce.3
